TPU v7x, 256 devices: a whole 4x4x8 slice. The times are simulated.
256 devices in a mesh: rep: 16 (over z, y_hi), exp: 16 (over y_lo, x, core).
Axes of the slice: x: 4, y: 4 (y_hi: 2, y_lo: 2; y = y_hi * 2 + y_lo), z: 8, core: 2. Of those that a mesh axis runs over, the one named last changes fastest.
Arguments:
- tokens: bfloat16 [8192, 2048], P(('rep', 'exp')), may hold values from -6 to 6
- attend_weight: bfloat16 [2048, 16, 256], P(None, 'exp'), may hold values from -0.125 to 0.125
- value_weight: bfloat16 [2048, 32, 256], P(None, 'exp'), may hold values from -0.125 to 0.125
- rate_weight: bfloat16 [2048, 32, 2], P(None, 'exp'), may hold values from -0.125 to 0.125
- decay_rate: float32 [32], P('exp'), may hold values from 0.002 to 0.2
- output_weight: bfloat16 [32, 128, 2048], P('exp'), may hold values from -0.09375 to 0.09375
- state_cache: float32 [128, 32, 128, 128], P('rep', 'exp'), may hold values from -2.4 to 2.4
- resume_from: int32 [128], replicated, may hold values from 0 to 127, as said below
- expert_index: int32 [8192, 10], P(('rep', 'exp')), may hold values from 0 to 15, all different within a row; in each aligned block of 32 rows (0 to 31, 32 to 63, ...) at most 32 rows name the same one
- route_weight: float32 [8192, 10], P(('rep', 'exp')), may hold values from 0.02 to 0.3
- expert_inner: bfloat16 [16, 2048, 1024], P('exp'), may hold values from -0.125 to 0.125
- expert_outer: bfloat16 [16, 512, 2048], P('exp'), may hold values from -0.25 to 0.25
Outputs:
- layer_output: bfloat16 [8192, 2048], P(('rep', 'exp'))
- final_state: float32 [128, 32, 128, 128], P('rep', 'exp')
Inputs may be any that keep to these rules, and one draw needn't show every extreme that they name: `resume_from`: entry r * 8 + b is the cache row of trajectory b of group r; cache row c belongs to group c // 8. The 8 trajectories of one group take their rows from 8 different groups; a row may serve several groups. `expert_index`: each row names 10 different experts.
All inputs are finite; a program needn't handle non-finite values.
Results may differ from a plain program's by a relative error of at most 0.013.
Values may be sent and summed in bfloat16 or wider, within the bound.
No kernel may reach another device: no remote copies, remote signals or barrier semaphores. Data moves between devices by JAX's collectives and lax.ppermute only.
A program may use at most 128 MiB of HBM per device.

v0:
```python
from functools import partial
import jax
import jax.numpy as jnp
from jax import lax
from jax.sharding import PartitionSpec as P

EPSILON = 1e-06
HIGHEST = lax.Precision.HIGHEST


def rms_scale(values):
    return values * lax.rsqrt(jnp.mean(values * values, axis=-1, keepdims=True) + EPSILON)


def unit_length(values):
    return values * lax.rsqrt(jnp.sum(values * values, axis=-1, keepdims=True) + EPSILON)


def head_inputs(attend_part, value_part, rate_part, key_heads, value_heads, decay_rate):
    count = attend_part.shape[0]
    key_size = attend_part.shape[1] // (2 * key_heads)
    value_size = value_part.shape[1] // (2 * value_heads)
    paired = attend_part.reshape(count, key_heads, 2, key_size)
    repeat = value_heads // key_heads
    query = jnp.repeat(unit_length(paired[:, :, 0]), repeat, axis=1) * key_size ** (-0.5)
    key_rows = jnp.repeat(unit_length(paired[:, :, 1]), repeat, axis=1)
    value_pair = value_part.reshape(count, value_heads, 2, value_size)
    rate_pair = rate_part.reshape(count, value_heads, 2)
    beta_rows = jax.nn.sigmoid(rate_pair[:, :, 1])
    log_decay = -decay_rate[None, :] * jax.nn.softplus(rate_pair[:, :, 0])
    return (query, key_rows, value_pair[:, :, 0], value_pair[:, :, 1], beta_rows, log_decay)


def block_step(state, packed):
    query, key_rows, value_rows, beta_rows, log_decay = packed
    summed = jnp.cumsum(log_decay, axis=-1)
    width = summed.shape[-1]
    row_iota = lax.broadcasted_iota(jnp.int32, (width, width), 0)
    col_iota = lax.broadcasted_iota(jnp.int32, (width, width), 1)
    spread = summed[..., :, None] - summed[..., None, :]
    ratio = jnp.where(col_iota <= row_iota, jnp.exp(jnp.minimum(spread, 0.0)), 0.0)
    key_products = jnp.einsum("bhik,bhjk->bhij", key_rows, key_rows, precision=HIGHEST)
    below = jnp.where(col_iota < row_iota, beta_rows[..., :, None] * ratio * key_products, 0.0)
    system = below + jnp.eye(width, dtype=jnp.float32)
    carried = jnp.einsum("bhik,bhvk->bhiv", key_rows, state, precision=HIGHEST)
    right_side = beta_rows[..., None] * (value_rows - jnp.exp(summed)[..., None] * carried)
    solver = jax.vmap(partial(jax.scipy.linalg.solve_triangular, lower=True, unit_diagonal=True))
    updates = solver(
        system.reshape(-1, width, width), right_side.reshape(-1, width, right_side.shape[-1])
    ).reshape(right_side.shape)
    query_keys = jnp.einsum("bhik,bhjk->bhij", query, key_rows, precision=HIGHEST)
    readout = jnp.exp(summed)[..., None] * jnp.einsum(
        "bhik,bhvk->bhiv", query, state, precision=HIGHEST
    )
    readout = readout + jnp.einsum(
        "bhij,bhjv->bhiv", ratio * query_keys, updates, precision=HIGHEST
    )
    closing = summed[..., -1:]
    tail = jnp.exp(closing - summed)
    new_state = jnp.exp(closing)[..., None] * state + jnp.einsum(
        "bhjv,bhjk->bhvk", updates * tail[..., None], key_rows, precision=HIGHEST
    )
    return (new_state, readout)


def local(
    tokens,
    attend_weight,
    value_weight,
    rate_weight,
    decay_rate,
    output_weight,
    state_cache,
    resume_from,
    expert_index,
    route_weight,
    expert_inner,
    expert_outer,
):
    model = tokens.shape[1]
    key_heads = attend_weight.shape[1]
    value_heads = value_weight.shape[1]
    attend_flat = attend_weight.reshape(model, -1)
    value_flat = value_weight.reshape(model, -1)
    rate_flat = rate_weight.reshape(model, -1)
    residual = tokens.astype(jnp.float32)
    normed = rms_scale(residual).astype(jnp.bfloat16)
    piece = lax.all_gather(normed, "exp", axis=0, tiled=True)
    projected = jnp.concatenate(
        [
            jnp.dot(piece, attend_flat, preferred_element_type=jnp.float32),
            jnp.dot(piece, value_flat, preferred_element_type=jnp.float32),
            jnp.dot(piece, rate_flat, preferred_element_type=jnp.float32),
        ],
        axis=1,
    )
    first_cut = attend_flat.shape[1]
    second_cut = first_cut + value_flat.shape[1]
    query, key_rows, value_rows, gate_rows, beta_rows, log_decay = head_inputs(
        projected[:, :first_cut],
        projected[:, first_cut:second_cut],
        projected[:, second_cut:],
        key_heads,
        value_heads,
        decay_rate,
    )
    trajs = state_cache.shape[0]
    myself = lax.axis_index("rep")
    my_rows = lax.dynamic_slice_in_dim(resume_from, myself * trajs, trajs)
    every_cache = lax.all_gather(
        state_cache.astype(jnp.bfloat16), "rep", axis=0, tiled=True
    ).astype(state_cache.dtype)
    start = jnp.take(every_cache, my_rows, axis=0)
    length = projected.shape[0] // trajs
    block = min(64, length)
    blocks = length // block

    def arrange(values):
        shaped = values.reshape((trajs, blocks, block) + values.shape[1:])
        return jnp.moveaxis(jnp.moveaxis(shaped, 3, 1), 2, 0)

    final_state, readout = lax.scan(
        block_step,
        start,
        (
            arrange(query),
            arrange(key_rows),
            arrange(value_rows),
            arrange(beta_rows),
            arrange(log_decay),
        ),
    )
    readout = jnp.transpose(readout, (1, 0, 3, 2, 4)).reshape(value_rows.shape)
    gated = (
        (rms_scale(readout) * jax.nn.silu(gate_rows))
        .astype(jnp.bfloat16)
        .reshape(readout.shape[0], -1)
    )
    output_flat = output_weight.reshape(-1, model)
    row_count = tokens.shape[0]
    attended = lax.psum_scatter(
        jnp.dot(gated, output_flat, preferred_element_type=jnp.float32).astype(jnp.bfloat16),
        "exp",
        scatter_dimension=0,
        tiled=True,
    ).astype(jnp.float32)
    hidden = residual + attended
    hidden_normed = rms_scale(hidden).astype(jnp.bfloat16)
    top_count = expert_index.shape[1]
    local_experts = expert_inner.shape[0]
    total_experts = lax.axis_size("exp") * local_experts
    flat_index = expert_index.reshape(-1)
    one_hot = (flat_index[:, None] == jnp.arange(total_experts, dtype=jnp.int32)[None, :]).astype(
        jnp.int32
    )
    earlier = jnp.cumsum(one_hot, axis=0) - one_hot
    slot_of_pair = jnp.sum(earlier * one_hot, axis=1)
    position = flat_index * row_count + slot_of_pair
    owner = jnp.arange(row_count * top_count, dtype=jnp.int32) // top_count
    table = jnp.full((total_experts * row_count,), row_count, jnp.int32).at[position].set(owner)
    padded = jnp.concatenate([hidden_normed, jnp.zeros((1, model), jnp.bfloat16)], axis=0)
    outgoing_rows = jnp.take(padded, table, axis=0).reshape(
        lax.axis_size("exp"), local_experts, row_count, model
    )
    inner = expert_outer.shape[1]
    both_parts = jnp.einsum(
        "semd,edf->semf",
        lax.all_to_all(outgoing_rows, "exp", split_axis=0, concat_axis=0, tiled=True),
        expert_inner,
        preferred_element_type=jnp.float32,
    )
    activated = (jax.nn.silu(both_parts[..., :inner]) * both_parts[..., inner:]).astype(
        jnp.bfloat16
    )
    produced = jnp.einsum(
        "semf,efd->semd", activated, expert_outer, preferred_element_type=jnp.float32
    ).astype(jnp.bfloat16)
    returned = lax.all_to_all(produced, "exp", split_axis=0, concat_axis=0, tiled=True)
    pair_output = jnp.take(
        returned.reshape(total_experts * row_count, model), position, axis=0
    ).reshape(row_count, top_count, model)
    expert_sum = jnp.einsum(
        "rt,rtd->rd", route_weight, pair_output.astype(jnp.float32), precision=HIGHEST
    )
    layer_output = (hidden + expert_sum).astype(jnp.bfloat16)
    return (layer_output, final_state)


def solution(mesh):
    in_specs = (
        P(("rep", "exp"), None),
        P(None, "exp", None),
        P(None, "exp", None),
        P(None, "exp", None),
        P("exp"),
        P("exp", None, None),
        P("rep", "exp", None, None),
        P(),
        P(("rep", "exp"), None),
        P(("rep", "exp"), None),
        P("exp", None, None),
        P("exp", None, None),
    )
    out_specs = (P(("rep", "exp"), None), P("rep", "exp", None, None))
    return jax.shard_map(local, mesh=mesh, in_specs=in_specs, out_specs=out_specs, check_vma=False)
```

profile of v0, /device:TPU:2, one launch (start us, length us, event | category | flops | bytes accessed | tf_op | source)
XLA Modules:
  0.0 379.0 jit_solution(10832503527195283775)
XLA Ops:
  12.3 3.4 copy.105
  15.7 4.1 %copy.84 = bf16[512,2048]{1,0:T(8,128)(2,1)} copy(bf16[512,2048]{0,1:T(8,128)(2,1)} %bitcast.128) | data formatting | bytes 4194304 | tf_op jit(solution)/shard_map/dot_general | solution.py:92
  21.5 27.9 %all-gather.3.cloned.1.call-done = bf16[512,2048]{1,0:T(8,128)(2,1)} async-done(((bf16[32,2048]{1,0:T(8,128)(2,1)}), bf16[512,2048]{1,0:T(8,128)(2,1)}) %all-gather.3.cloned.1.call-update) | async-done | bytes 2097168 | tf_op jit(solution)/shard_map/all_gather | solution.py:88
  49.4 2.6 fusion.22
  55.3 3.5 fusion.3
  64.0 80.0 %custom-call.5 = f32[16,1,64,64]{2,3,1,0:T(8,128)} custom-call(f32[16,1,64,64]{3,2,1,0:T(8,128)} %select_add_fusion), custom_call_target="InvertDiagBlocksLowerTriangular" | custom-call | tf_op jit(solution)/shard_map/while/body/eval_jaxpr/vmap(jit(_solve_triangular))/triangular_solve | solution.py:48
  145.9 42.7 %all-gather.5.cloned.1.call-done = bf16[128,2,128,128]{3,2,1,0:T(8,128)(2,1)} async-done(((bf16[8,2,128,128]{3,2,1,0:T(8,128)(2,1)}), bf16[128,2,128,128]{3,2,1,0:T(8,128)(2,1)}) %all-gather.5.cloned.1.call-update) | async-done | bytes 8388624 | tf_op jit(solution)/shard_map/all_gather | solution.py:110
  188.7 11.2 %convert_element_type.58 = f32[128,2,128,128]{3,2,1,0:T(8,128)} convert(bf16[128,2,128,128]{3,2,1,0:T(8,128)(2,1)} %all-gather.5.cloned.1.call-done) | non-fusion elementwise | flops 4194304 | bytes 25165824 | tf_op jit(solution)/shard_map/convert_element_type | solution.py:112
  199.9 6.4 %gather_fusion = f32[8,2,128,128]{3,2,1,0:T(8,128)S(1)} fusion(f32[128,2,128,128]{3,2,1,0:T(8,128)} %convert_element_type.58, s32[1024]{0:T(1024)S(1)} %pad_clamp_fusion.2), kind=kCustom, calls=%fused_computation | custom fusion | bytes 2097184 | tf_op jit(solution)/shard_map/jit(_take)/gather | solution.py:113
  206.3 3.3 fusion.27
  212.2 2.3 multiply_reduce_fusion
  215.4 3.7 bitcast_convert_fusion
  221.4 2.9 scatter_custom_fusion
  224.5 54.1 %reduce-scatter.2.cloned.1.call-done = bf16[32,2048]{1,0:T(8,128)(2,1)} async-done(((bf16[512,2048]{1,0:T(8,128)(2,1)}), bf16[32,2048]{1,0:T(8,128)(2,1)}) %reduce-scatter.2.cloned.1.call-update) | async-done | bytes 131088 | tf_op jit(solution)/shard_map/reduce_scatter | solution.py:141
  280.6 3.3 gather_fusion.1
  285.8 31.6 %all_to_all.10 = bf16[16,1,32,2048]{3,2,1,0:T(8,128)(2,1)S(1)} all-to-all(bf16[16,1,32,2048]{3,2,1,0:T(8,128)(2,1)S(1)} %broadcast_select_fusion), channel_id=1, replica_groups=mesh['rep'=16,'exp'=16] {'exp'}, dimensions={0} | all-to-all | bytes 4194304 | tf_op jit(solution)/shard_map/all_to_all | solution.py:168
  317.5 2.4 fusion.14
  319.9 2.6 fusion.2
  322.5 7.7 %all-to-all-start.1 = ((bf16[16,1,32,2048]{3,2,1,0:T(8,128)(2,1)}), bf16[16,1,32,2048]{3,2,1,0:T(8,128)(2,1)}, u32[]{:S(2)}, u32[]{:S(2)}) async-start(bf16[16,1,32,2048]{3,2,1,0:T(8,128)(2,1)} %fusion.2), calls=%async_computation.2 | async-start | bytes 4194304 | tf_op jit(solution)/shard_map/all_to_all | solution.py:178
  337.0 4.0 %convolution_add_fusion = f32[8,2,128,128]{3,2,1,0:T(8,128)} fusion(f32[8,2,128,128]{3,2,1,0:T(8,128)S(1)} %gather_fusion, f32[8,2,64,128]{3,2,1,0:T(8,128)} %bitcast.130, f32[8,2]{1,0:T(8,128)S(1)} %bitcast.143, pred[8]{0:T(512)(128)(4,1)} %copy-done.18, f32[8,2,64]{2,1,0:T(2,128)S(1)} %copy.96, f32[8,64,128]{2,1,0:T(8,128)S(1)} %copy-done.3), kind=kOutput, calls=%fused_computation.22 | convolution fusion | flops 202244096 | bytes 2887752 | tf_op jit(solution)/shard_map/while/body/eval_jaxpr/bhjv,bhjk->bhvk/dot_general | solution.py:60
  341.0 17.7 %all-to-all-done.1 = bf16[16,1,32,2048]{3,2,1,0:T(8,128)(2,1)} async-done(((bf16[16,1,32,2048]{3,2,1,0:T(8,128)(2,1)}), bf16[16,1,32,2048]{3,2,1,0:T(8,128)(2,1)}, u32[]{:S(2)}, u32[]{:S(2)}) %all-to-all-start.1) | async-done | bytes 2097184 | tf_op jit(solution)/shard_map/all_to_all | solution.py:178
  358.8 6.8 %gather_fusion.2 = bf16[320,2048]{1,0:T(8,128)(2,1)} fusion(bf16[512,2048]{1,0:T(8,128)(2,1)} %bitcast.48, s32[1024]{0:T(1024)S(1)} %copy-done.15), kind=kCustom, calls=%fused_computation.2 | custom fusion | bytes 2622720 | tf_op jit(solution)/shard_map/jit(_take)/gather | solution.py:179
  365.6 3.4 gather.20
  369.0 2.7 fusion.11
  (121 shorter events, 34.5 us)
Async XLA Ops:
  7.2 312.7 %copy-start = (bf16[1,512,2048]{2,1,0:T(8,128)(2,1)S(1)}, bf16[1,512,2048]{2,1,0:T(8,128)(2,1)}, u32[]{:S(2)}) copy-start(bf16[1,512,2048]{2,1,0:T(8,128)(2,1)} %param.23) | copy-start | bytes 6291460
  7.2 42.2 %all-gather.3.cloned.1.call-start = ((), (), s32[]{:S(2)}) async-start(), calls=%async_computation.3 | async-start | bytes 2228224 | tf_op jit(solution)/shard_map/all_gather | solution.py:88
  10.1 178.6 %all-gather.5.cloned.1.call-start = ((), (), s32[]{:S(2)}) async-start(), calls=%async_computation.4 | async-start | bytes 8912896 | tf_op jit(solution)/shard_map/all_gather | solution.py:110
  12.3 266.2 %reduce-scatter.2.cloned.1.call-start = ((), (), s32[]{:S(2)}) async-start(), calls=%async_computation.5 | async-start | bytes 2228224 | tf_op jit(solution)/shard_map/reduce_scatter | solution.py:141
  15.7 4.1 %copy-start.9 = (bf16[2048,1,256]{2,0,1:T(8,128)(2,1)S(1)}, bf16[2048,1,256]{2,0,1:T(8,128)(2,1)}, u32[]{:S(2)}) copy-start(bf16[2048,1,256]{2,0,1:T(8,128)(2,1)} %param.13) | copy-start | bytes 3145732
  19.8 1.4 copy-start.14
  19.8 1.5 copy-start.22
  19.8 1.5 copy-start.20
  21.4 190.8 %copy-start.18 = (pred[8]{0:T(512)(128)(4,1)}, pred[8]{0:T(512)(128)(4,1)S(1)}, u32[]{:S(2)}) copy-start(pred[8]{0:T(512)(128)(4,1)S(1)} %get-tuple-element.22) | copy-start | bytes 28
  62.2 144.1 %copy-start.2 = (f32[8,64,128]{2,1,0:T(8,128)}, f32[8,64,128]{2,1,0:T(8,128)S(1)}, u32[]{:S(2)}) copy-start(f32[8,64,128]{2,1,0:T(8,128)S(1)} %broadcast_multiply_fusion) | copy-start | bytes 786436
  144.2 44.5 %copy-start.5 = (f32[8,64,128]{2,1,0:T(8,128)}, f32[8,64,128]{2,1,0:T(8,128)S(1)}, u32[]{:S(2)}) copy-start(f32[8,64,128]{2,1,0:T(8,128)S(1)} %multiply_multiply_fusion) | copy-start | bytes 786436
  206.3 3.4 copy-start.10
  206.3 5.2 %copy-start.7 = (f32[8,2,64,64]{3,2,1,0:T(8,128)S(1)}, f32[8,2,64,64]{3,2,1,0:T(8,128)}, u32[]{:S(2)}) copy-start(f32[8,2,64,64]{3,2,1,0:T(8,128)} %convolution_multiply_fusion.3) | copy-start | bytes 786436
  209.6 2.5 copy-start.6
  219.1 59.5 %copy-start.4 = (bf16[32,2048]{1,0:T(8,128)(2,1)S(1)}, bf16[32,2048]{1,0:T(8,128)(2,1)}, u32[]{:S(2)}) copy-start(bf16[32,2048]{1,0:T(8,128)(2,1)} %param.12) | copy-start | bytes 393220
  221.4 58.2 %copy-start.12 = (s32[320]{0:T(512)}, s32[320]{0:T(512)S(1)}, u32[]{:S(2)}) copy-start(s32[320]{0:T(512)S(1)} %fusion.56) | copy-start | bytes 3844
  221.4 2.9 copy-start.17
  285.8 31.7 %copy-start.21 = (bf16[1,2048,1024]{2,1,0:T(8,128)(2,1)S(1)}, bf16[1,2048,1024]{2,1,0:T(8,128)(2,1)}, u32[]{:S(2)}) copy-start(bf16[1,2048,1024]{2,1,0:T(8,128)(2,1)} %param.22) | copy-start | bytes 12582916
  322.5 14.5 %copy-start.3 = (f32[8,64,128]{2,1,0:T(8,128)S(1)}, f32[8,64,128]{2,1,0:T(8,128)}, u32[]{:S(2)}) copy-start(f32[8,64,128]{2,1,0:T(8,128)} %copy-done.2) | copy-start | bytes 786436
  322.5 36.3 %all-to-all-start.1 = ((bf16[16,1,32,2048]{3,2,1,0:T(8,128)(2,1)}), bf16[16,1,32,2048]{3,2,1,0:T(8,128)(2,1)}, u32[]{:S(2)}, u32[]{:S(2)}) async-start(bf16[16,1,32,2048]{3,2,1,0:T(8,128)(2,1)} %fusion.2), calls=%async_computation.2 | async-start | bytes 4194304 | tf_op jit(solution)/shard_map/all_to_all | solution.py:178
  335.4 23.3 %copy-start.15 = (s32[1024]{0:T(1024)S(1)}, s32[1024]{0:T(1024)}, u32[]{:S(2)}) copy-start(s32[1024]{0:T(1024)} %pad_clamp_fusion) | copy-start | bytes 12292
  365.6 3.4 copy-start.13
  365.6 3.4 copy-start.19
  369.0 2.7 copy-start.8
  (3 other events, 2.5 us)
Sparse Core Ops, SparseCore 0:
  10.4 38.9 all-gather.2
  52.0 136.6 all-gather.4
  219.2 59.2 reduce-scatter.1
where the time goes:
time: 380 us; the launch traced here: 379 us
  waiting for transfers between devices  142 us (37%)
  other arithmetic  107 us (28%)
  local copies, waits for them, and re-layouts  41.9 us (11%)
  matrix products  33.8 us (9%)
  blocking collectives  31.6 us (8%)
  between operations  14.2 us (4%)
  starting transfers between devices  7.8 us (2%)
    another operation x4, other arithmetic, block_step(): solver(system.reshape(-1, width, width), right_side.reshape(-1, width, ri...  80.9 us
    reduce_scatter x1, waiting for transfers between devices, local(): lax.psum_scatter(jnp.dot(gated, output_flat, preferred_element_type=jnp.f...  54.1 us
    all_gather x1, waiting for transfers between devices, local(): lax.all_gather(state_cache.astype(jnp.bfloat16), 'rep', axis=0, tiled=True)  42.7 us
    all_to_all x1, blocking collectives, local(): lax.all_to_all(outgoing_rows, 'exp', split_axis=0, concat_axis=0, tiled=T...  31.6 us
    all_gather x1, waiting for transfers between devices, local(): piece = lax.all_gather(normed, 'exp', axis=0, tiled=True)  27.9 us
    all_to_all x1, waiting for transfers between devices, local(): lax.all_to_all(produced, 'exp', split_axis=0, concat_axis=0, tiled=True)  17.7 us
    convert_element_type x1, other arithmetic, local(): every_cache = lax.all_gather(state_cache.astype(jnp.bfloat16), 'rep', axi...  11.2 us
    gather x2, local copies, waits for them, and re-layouts, local(): jnp.take(returned.reshape(total_experts * row_count, model), position, ax...  10.2 us
  transfers between devices with their start and end apart: 4, of which 4 were waited for; matrix products, arithmetic and copies ran while one was open for 32% of the time, Pallas kernels for 0%

commit v1 on v0

--- a/solution.py
+++ b/solution.py
@@ -85,7 +85,9 @@
     rate_flat = rate_weight.reshape(model, -1)
     residual = tokens.astype(jnp.float32)
     normed = rms_scale(residual).astype(jnp.bfloat16)
-    piece = lax.all_gather(normed, "exp", axis=0, tiled=True)
+    piece = jnp.concatenate(
+        lax.all_to_all(jnp.stack([normed] * lax.axis_size("exp")), "exp", 0, 0), axis=0
+    )
     projected = jnp.concatenate(
         [
             jnp.dot(piece, attend_flat, preferred_element_type=jnp.float32),

time: 380 us -> 357 us (0.939)
  waiting for transfers between devices: 142 us -> 107 us
  starting transfers between devices: 7.8 us -> 14.2 us
    all_gather x1 -> x0, waiting for transfers between devices: 27.9 us -> none  [local(): piece = lax.all_gather(normed, 'exp', axis=0, tiled=True)]
    all_gather x1, waiting for transfers between devices: 42.7 us -> 18.2 us  [local(): lax.all_gather(state_cache.astype(jnp.bfloat16), 'rep', axis=0, tiled=True)]
    all_to_all x0 -> x1, waiting for transfers between devices: none -> 16.7 us  [local(): lax.all_to_all(jnp.stack([normed] * lax.axis_size('exp')), 'exp', 0, 0)]
    all_to_all x0 -> x1, starting transfers between devices: none -> 6.4 us  [local(): lax.all_to_all(jnp.stack([normed] * lax.axis_size('exp')), 'exp', 0, 0)]
  transfers between devices with their start and end apart: 4 -> 4, of which waited for: 4 -> 4; matrix products, arithmetic and copies ran while one was open for 32% -> 36% of each run, Pallas kernels for 0% -> 0%
where the time goes in v1:
time: 357 us; the launch traced here: 356 us
  other arithmetic  109 us (31%)
  waiting for transfers between devices  107 us (30%)
  local copies, waits for them, and re-layouts  44.2 us (12%)
  matrix products  35.4 us (10%)
  blocking collectives  31.7 us (9%)
  between operations  14.5 us (4%)
  starting transfers between devices  14.2 us (4%)
    another operation x4, other arithmetic, block_step(): solver(system.reshape(-1, width, width), right_side.reshape(-1, width, ri...  82.4 us
    reduce_scatter x1, waiting for transfers between devices, local(): lax.psum_scatter(jnp.dot(gated, output_flat, preferred_element_type=jnp.f...  54.1 us
    all_to_all x1, blocking collectives, local(): lax.all_to_all(outgoing_rows, 'exp', split_axis=0, concat_axis=0, tiled=T...  31.7 us
    all_gather x1, waiting for transfers between devices, local(): lax.all_gather(state_cache.astype(jnp.bfloat16), 'rep', axis=0, tiled=True)  18.2 us
    all_to_all x1, waiting for transfers between devices, local(): lax.all_to_all(produced, 'exp', split_axis=0, concat_axis=0, tiled=True)  17.7 us
    all_to_all x1, waiting for transfers between devices, local(): lax.all_to_all(jnp.stack([normed] * lax.axis_size('exp')), 'exp', 0, 0)  16.7 us
    convert_element_type x1, other arithmetic, local(): every_cache = lax.all_gather(state_cache.astype(jnp.bfloat16), 'rep', axi...  11.2 us
    gather x2, local copies, waits for them, and re-layouts, local(): jnp.take(returned.reshape(total_experts * row_count, model), position, ax...  10.2 us
  transfers between devices with their start and end apart: 4, of which 4 were waited for; matrix products, arithmetic and copies ran while one was open for 36% of the time, Pallas kernels for 0%

profile of v1, /device:TPU:2, one launch (start us, length us, event | category | flops | bytes accessed | tf_op | source)
XLA Modules:
  0.0 355.9 jit_solution(14142221025996828993)
XLA Ops:
  11.4 6.4 %all-to-all-start = ((bf16[16,32,2048]{2,1,0:T(8,128)(2,1)}), bf16[16,32,2048]{2,1,0:T(8,128)(2,1)}, u32[]{:S(2)}, u32[]{:S(2)}) async-start(bf16[16,32,2048]{2,1,0:T(8,128)(2,1)} %stack.2), calls=%async_computation | async-start | bytes 4194304 | tf_op jit(solution)/shard_map/all_to_all | solution.py:89
  17.8 3.4 copy.105
  21.2 4.0 %copy.84 = bf16[512,2048]{1,0:T(8,128)(2,1)} copy(bf16[512,2048]{0,1:T(8,128)(2,1)} %bitcast.126) | data formatting | bytes 4194304 | tf_op jit(solution)/shard_map/dot_general | solution.py:94
  29.9 16.7 %all-to-all-done = bf16[16,32,2048]{2,1,0:T(8,128)(2,1)} async-done(((bf16[16,32,2048]{2,1,0:T(8,128)(2,1)}), bf16[16,32,2048]{2,1,0:T(8,128)(2,1)}, u32[]{:S(2)}, u32[]{:S(2)}) %all-to-all-start) | async-done | bytes 2097184 | tf_op jit(solution)/shard_map/all_to_all | solution.py:89
  46.5 2.6 convolution_bitcast_fusion
  53.0 3.5 fusion.68
  63.5 80.0 %custom-call.5 = f32[16,1,64,64]{2,3,1,0:T(8,128)} custom-call(f32[16,1,64,64]{3,2,1,0:T(8,128)} %select_add_fusion), custom_call_target="InvertDiagBlocksLowerTriangular" | custom-call | tf_op jit(solution)/shard_map/while/body/eval_jaxpr/vmap(jit(_solve_triangular))/triangular_solve | solution.py:48
  144.4 2.5 convolution_multiply_fusion.3
  146.8 18.2 %all-gather.2.cloned.1.call-done = bf16[128,2,128,128]{3,2,1,0:T(8,128)(2,1)} async-done(((bf16[8,2,128,128]{3,2,1,0:T(8,128)(2,1)}), bf16[128,2,128,128]{3,2,1,0:T(8,128)(2,1)}) %all-gather.2.cloned.1.call-update) | async-done | bytes 8388624 | tf_op jit(solution)/shard_map/all_gather | solution.py:112
  165.1 11.2 %convert_element_type.58 = f32[128,2,128,128]{3,2,1,0:T(8,128)} convert(bf16[128,2,128,128]{3,2,1,0:T(8,128)(2,1)} %all-gather.2.cloned.1.call-done) | non-fusion elementwise | flops 4194304 | bytes 25165824 | tf_op jit(solution)/shard_map/convert_element_type | solution.py:114
  176.3 6.5 %gather_fusion = f32[8,2,128,128]{3,2,1,0:T(8,128)S(1)} fusion(f32[128,2,128,128]{3,2,1,0:T(8,128)} %convert_element_type.58, s32[1024]{0:T(1024)} %pad_clamp_fusion.2), kind=kCustom, calls=%fused_computation | custom fusion | bytes 2097184 | tf_op jit(solution)/shard_map/jit(_take)/gather | solution.py:115
  182.9 3.3 fusion.18
  192.0 3.7 %bitcast_convert_fusion = bf16[512,2048]{1,0:T(8,128)(2,1)} fusion(bf16[2,128,2048]{2,1,0:T(8,128)(2,1)} %param.17, f32[512,2,2,128]{3,0,2,1:T(8,128)} %copy-done.11, f32[512,2,128]{2,0,1:T(8,128)} %bitcast.137, f32[512,2]{0,1:T(2,128)S(1)} %rsqrt.57), kind=kOutput, calls=%fused_computation.6 | convolution fusion | flops 538836992 | bytes 4198400 | tf_op jit(solution)/shard_map/dot_general | solution.py:144
  198.0 2.9 scatter_custom_fusion
  201.0 54.1 %reduce-scatter.2.cloned.1.call-done = bf16[32,2048]{1,0:T(8,128)(2,1)} async-done(((bf16[512,2048]{1,0:T(8,128)(2,1)}), bf16[32,2048]{1,0:T(8,128)(2,1)}) %reduce-scatter.2.cloned.1.call-update) | async-done | bytes 131088 | tf_op jit(solution)/shard_map/reduce_scatter | solution.py:143
  257.3 3.3 gather_fusion.1
  262.5 31.7 %all_to_all.15 = bf16[16,1,32,2048]{3,2,1,0:T(8,128)(2,1)S(1)} all-to-all(bf16[16,1,32,2048]{3,2,1,0:T(8,128)(2,1)S(1)} %broadcast_select_fusion), channel_id=1, replica_groups=mesh['rep'=16,'exp'=16] {'exp'}, dimensions={0} | all-to-all | bytes 4194304 | tf_op jit(solution)/shard_map/all_to_all | solution.py:170
  296.5 2.6 fusion.2
  299.1 7.7 %all-to-all-start.2 = ((bf16[16,1,32,2048]{3,2,1,0:T(8,128)(2,1)}), bf16[16,1,32,2048]{3,2,1,0:T(8,128)(2,1)}, u32[]{:S(2)}, u32[]{:S(2)}) async-start(bf16[16,1,32,2048]{3,2,1,0:T(8,128)(2,1)} %fusion.2), calls=%async_computation.3 | async-start | bytes 4194304 | tf_op jit(solution)/shard_map/all_to_all | solution.py:180
  313.6 4.0 %convolution_add_fusion = f32[8,2,128,128]{3,2,1,0:T(8,128)} fusion(f32[8,2,128,128]{3,2,1,0:T(8,128)S(1)} %gather_fusion, f32[8,2,64,128]{3,2,1,0:T(8,128)} %bitcast.128, f32[8,2]{1,0:T(8,128)S(1)} %bitcast.141, pred[8]{0:T(512)(128)(4,1)} %get-tuple-element.22, f32[8,2,64]{2,1,0:T(2,128)S(1)} %copy.96, f32[8,64,128]{2,1,0:T(8,128)S(1)} %copy-done.3), kind=kOutput, calls=%fused_computation.16 | convolution fusion | flops 202244096 | bytes 2887752 | tf_op jit(solution)/shard_map/while/body/eval_jaxpr/bhjv,bhjk->bhvk/dot_general | solution.py:60
  317.7 17.7 %all-to-all-done.2 = bf16[16,1,32,2048]{3,2,1,0:T(8,128)(2,1)} async-done(((bf16[16,1,32,2048]{3,2,1,0:T(8,128)(2,1)}), bf16[16,1,32,2048]{3,2,1,0:T(8,128)(2,1)}, u32[]{:S(2)}, u32[]{:S(2)}) %all-to-all-start.2) | async-done | bytes 2097184 | tf_op jit(solution)/shard_map/all_to_all | solution.py:180
  335.4 6.8 %gather_fusion.2 = bf16[320,2048]{1,0:T(8,128)(2,1)} fusion(bf16[512,2048]{1,0:T(8,128)(2,1)} %bitcast.50, s32[1024]{0:T(1024)S(1)} %copy-done.17), kind=kCustom, calls=%fused_computation.2 | custom fusion | bytes 2622720 | tf_op jit(solution)/shard_map/jit(_take)/gather | solution.py:181
  342.3 3.4 gather.20
  345.6 2.7 fusion.5
  (125 shorter events, 42.4 us)
Async XLA Ops:
  7.2 289.4 %copy-start = (bf16[1,512,2048]{2,1,0:T(8,128)(2,1)S(1)}, bf16[1,512,2048]{2,1,0:T(8,128)(2,1)}, u32[]{:S(2)}) copy-start(bf16[1,512,2048]{2,1,0:T(8,128)(2,1)} %param.23) | copy-start | bytes 6291460
  7.2 2.4 copy-start.4
  7.2 157.9 %all-gather.2.cloned.1.call-start = ((), (), s32[]{:S(2)}) async-start(), calls=%async_computation.4 | async-start | bytes 8912896 | tf_op jit(solution)/shard_map/all_gather | solution.py:112
  11.4 35.1 %all-to-all-start = ((bf16[16,32,2048]{2,1,0:T(8,128)(2,1)}), bf16[16,32,2048]{2,1,0:T(8,128)(2,1)}, u32[]{:S(2)}, u32[]{:S(2)}) async-start(bf16[16,32,2048]{2,1,0:T(8,128)(2,1)} %stack.2), calls=%async_computation | async-start | bytes 4194304 | tf_op jit(solution)/shard_map/all_to_all | solution.py:89
  17.8 237.4 %reduce-scatter.2.cloned.1.call-start = ((), (), s32[]{:S(2)}) async-start(), calls=%async_computation.5 | async-start | bytes 2228224 | tf_op jit(solution)/shard_map/reduce_scatter | solution.py:143
  21.2 4.0 %copy-start.9 = (bf16[2048,1,256]{2,0,1:T(8,128)(2,1)S(1)}, bf16[2048,1,256]{2,0,1:T(8,128)(2,1)}, u32[]{:S(2)}) copy-start(bf16[2048,1,256]{2,0,1:T(8,128)(2,1)} %param.13) | copy-start | bytes 3145732
  25.3 1.5 copy-start.22
  58.5 1.5 copy-start.12
  60.0 122.9 %copy-start.2 = (f32[8,64,128]{2,1,0:T(8,128)}, f32[8,64,128]{2,1,0:T(8,128)S(1)}, u32[]{:S(2)}) copy-start(f32[8,64,128]{2,1,0:T(8,128)S(1)} %broadcast_multiply_fusion) | copy-start | bytes 786436
  144.4 20.7 %copy-start.5 = (f32[8,64,128]{2,1,0:T(8,128)}, f32[8,64,128]{2,1,0:T(8,128)S(1)}, u32[]{:S(2)}) copy-start(f32[8,64,128]{2,1,0:T(8,128)S(1)} %multiply_multiply_fusion) | copy-start | bytes 786436
  176.3 6.6 %copy-start.13 = (f32[8,2,64]{2,1,0:T(2,128)S(1)}, f32[8,2,64]{2,1,0:T(2,128)}, u32[]{:S(2)}) copy-start(f32[8,2,64]{2,1,0:T(2,128)} %copy-done.12) | copy-start | bytes 12292
  182.8 3.4 copy-start.10
  182.8 5.2 %copy-start.7 = (f32[8,2,64,64]{3,2,1,0:T(8,128)S(1)}, f32[8,2,64,64]{3,2,1,0:T(8,128)}, u32[]{:S(2)}) copy-start(f32[8,2,64,64]{3,2,1,0:T(8,128)} %convolution_multiply_fusion.3) | copy-start | bytes 786436
  186.2 2.5 copy-start.6
  186.2 2.5 copy-start.20
  197.9 58.3 %copy-start.14 = (s32[320]{0:T(512)}, s32[320]{0:T(512)S(1)}, u32[]{:S(2)}) copy-start(s32[320]{0:T(512)S(1)} %fusion.47) | copy-start | bytes 3844
  198.0 2.9 copy-start.19
  262.5 31.7 %copy-start.23 = (bf16[1,2048,1024]{2,1,0:T(8,128)(2,1)S(1)}, bf16[1,2048,1024]{2,1,0:T(8,128)(2,1)}, u32[]{:S(2)}) copy-start(bf16[1,2048,1024]{2,1,0:T(8,128)(2,1)} %param.22) | copy-start | bytes 12582916
  299.1 14.5 %copy-start.3 = (f32[8,64,128]{2,1,0:T(8,128)S(1)}, f32[8,64,128]{2,1,0:T(8,128)}, u32[]{:S(2)}) copy-start(f32[8,64,128]{2,1,0:T(8,128)} %copy-done.2) | copy-start | bytes 786436
  299.1 36.3 %all-to-all-start.2 = ((bf16[16,1,32,2048]{3,2,1,0:T(8,128)(2,1)}), bf16[16,1,32,2048]{3,2,1,0:T(8,128)(2,1)}, u32[]{:S(2)}, u32[]{:S(2)}) async-start(bf16[16,1,32,2048]{3,2,1,0:T(8,128)(2,1)} %fusion.2), calls=%async_computation.3 | async-start | bytes 4194304 | tf_op jit(solution)/shard_map/all_to_all | solution.py:180
  312.1 23.3 %copy-start.17 = (s32[1024]{0:T(1024)S(1)}, s32[1024]{0:T(1024)}, u32[]{:S(2)}) copy-start(s32[1024]{0:T(1024)} %pad_clamp_fusion) | copy-start | bytes 12292
  342.2 3.4 copy-start.15
  342.3 3.4 copy-start.21
  345.6 2.7 copy-start.8
  (5 other events, 5.4 us)
Sparse Core Ops, SparseCore 0:
  10.6 154.4 all-gather.1
  195.8 59.3 reduce-scatter.1
